TPU v7x, 32 devices: a whole 2x2x4 slice. The times are simulated.
32 devices in a mesh: ctx: 8 (over z, core), wt: 4 (over y, x).
Axes of the slice: x: 2, y: 2, z: 4, core: 2. Of those that a mesh axis runs over, the one named last changes fastest.
Arguments:
- tokens: bfloat16 [4, 2048, 1024], P('wt', 'ctx'), may hold values from -6 to 6
- cotangent: bfloat16 [4, 2048, 1024], P('wt', 'ctx'), may hold values from -6 to 6
- ln1_gain: bfloat16 [1024], P('wt'), may hold values from 0.25 to 1.75
- ln1_bias: bfloat16 [1024], P('wt'), may hold values from -3 to 3
- w_qkv: bfloat16 [1024, 3072], P('wt'), may hold values from -0.1875 to 0.1875
- bias_q: bfloat16 [1024], P('wt'), may hold values from -3 to 3
- bias_v: bfloat16 [1024], P('wt'), may hold values from -1.25 to 1.25
- w_out: bfloat16 [1024, 1024], P('wt'), may hold values from -0.75 to 0.75
- bias_out: bfloat16 [1024], P('wt'), may hold values from -3 to 3
- ln2_gain: bfloat16 [1024], P('wt'), may hold values from 0.25 to 1.75
- ln2_bias: bfloat16 [1024], P('wt'), may hold values from -3 to 3
- w_up: bfloat16 [1024, 4096], P('wt'), may hold values from -0.1875 to 0.1875
- bias_up: bfloat16 [4096], P('wt'), may hold values from -3 to 3
- w_down: bfloat16 [4096, 1024], P('wt'), may hold values from -0.09375 to 0.09375
- bias_down: bfloat16 [1024], P('wt'), may hold values from -3 to 3
Outputs:
- out: bfloat16 [4, 2048, 1024], P('wt', 'ctx')
- grad_tokens: float32 [4, 2048, 1024], P('wt', 'ctx')
- grad_ln1_gain: float32 [1024], P('wt')
- grad_ln1_bias: float32 [1024], P('wt')
- grad_w_qkv: float32 [1024, 3072], P('wt')
- grad_bias_q: float32 [1024], P('wt')
- grad_bias_v: float32 [1024], P('wt')
- grad_w_out: float32 [1024, 1024], P('wt')
- grad_bias_out: float32 [1024], P('wt')
- grad_ln2_gain: float32 [1024], P('wt')
- grad_ln2_bias: float32 [1024], P('wt')
- grad_w_up: float32 [1024, 4096], P('wt')
- grad_bias_up: float32 [4096], P('wt')
- grad_w_down: float32 [4096, 1024], P('wt')
- grad_bias_down: float32 [1024], P('wt')
All inputs are finite; a program needn't handle non-finite values.
Results may differ from a plain program's by a relative error of at most 0.02.
Values may be sent and summed in bfloat16 or wider, within the bound.
A program may use at most 192 MiB of HBM per device.

v0:
```python
import jax
import jax.numpy as jnp
from jax import lax
from jax.sharding import PartitionSpec as P

HEADS = 16
HEAD_DIM = 64


EPSILON = 1e-05
MASKED_SCORE = -1e30


def from_behind(value, axis, steps):
    count = lax.axis_size(axis)
    pairs = [(source, (source + steps) % count) for source in range(count)]
    return lax.ppermute(value, axis, pairs)


def norm_rows(values_in, gain, shift):
    mean_val = jnp.mean(values_in, axis=-1, keepdims=True)
    centred = values_in - mean_val
    spread = jnp.mean(centred * centred, axis=-1, keepdims=True)
    return centred * lax.rsqrt(spread + EPSILON) * gain + shift


def gelu_tanh(values_in):
    return jax.nn.gelu(values_in, approximate=True)


def product(left, right):
    return jnp.dot(left, right, preferred_element_type=jnp.float32)


def product_left(left, right):
    return lax.dot_general(
        left, right, (((0,), (0,)), ((), ())), preferred_element_type=jnp.float32
    )


def product_right(left, right):
    return lax.dot_general(
        left, right, (((1,), (1,)), ((), ())), preferred_element_type=jnp.float32
    )


def half_positions(device, cycle_size, half_rows):
    offsets = jnp.arange(half_rows, dtype=jnp.int32)
    first = device * half_rows + offsets
    second = (2 * cycle_size - 1 - device) * half_rows + offsets
    return jnp.stack([first, second])


def pick(stacked, which_half):
    return lax.dynamic_index_in_dim(stacked, which_half, 0, keepdims=False)


def put_add(stacked, which_half, addend):
    return lax.dynamic_update_index_in_dim(
        stacked, pick(stacked, which_half) + addend, which_half, 0
    )


def head_split(half_block):
    return half_block.reshape(half_block.shape[0], HEADS, HEAD_DIM)


def pair_scores(query_half, key_half, query_pos, key_pos):
    scores = jnp.einsum(
        "qhd,khd->hqk",
        head_split(query_half),
        head_split(key_half),
        preferred_element_type=jnp.float32,
    )
    scores = scores * HEAD_DIM ** (-0.5)
    allowed = key_pos[None, :] <= query_pos[:, None]
    return jnp.where(allowed[None], scores, MASKED_SCORE)


def absorb(state, which_half, queries, query_pos, key_half, value_half, key_pos):
    peaks, totals, sums = state
    peak_old = pick(peaks, which_half)
    scores = pair_scores(pick(queries, which_half), key_half, pick(query_pos, which_half), key_pos)
    peak_new = jnp.maximum(peak_old, jnp.max(scores, axis=-1))
    fade = jnp.exp(peak_old - peak_new)
    prob_blk = jnp.exp(scores - peak_new[..., None])
    total_new = pick(totals, which_half) * fade + jnp.sum(prob_blk, axis=-1)
    sum_new = pick(sums, which_half) * fade[..., None] + jnp.einsum(
        "hqk,khd->hqd",
        prob_blk.astype(jnp.bfloat16),
        head_split(value_half),
        preferred_element_type=jnp.float32,
    )
    return (
        lax.dynamic_update_index_in_dim(peaks, peak_new, which_half, 0),
        lax.dynamic_update_index_in_dim(totals, total_new, which_half, 0),
        lax.dynamic_update_index_in_dim(sums, sum_new, which_half, 0),
    )


def pass_grads(grad_keys, grad_values):
    return (
        from_behind(grad_keys.astype(jnp.bfloat16), "ctx", 1).astype(grad_keys.dtype),
        from_behind(grad_values.astype(jnp.bfloat16), "ctx", 1).astype(grad_values.dtype),
    )


def per_device(
    tokens,
    cotangent,
    ln1_gain,
    ln1_bias,
    w_qkv,
    bias_q,
    bias_v,
    w_out,
    bias_out,
    ln2_gain,
    ln2_bias,
    w_up,
    bias_up,
    w_down,
    bias_down,
):
    (
        gain_attn,
        shift_attn,
        whole_qkv,
        query_bias,
        value_bias,
        whole_out,
        out_bias,
        gain_ffn,
        shift_ffn,
        whole_up,
        up_bias,
        whole_down,
        down_bias,
    ) = (
        lax.all_gather(ln1_gain, "wt", axis=0, tiled=True),
        lax.all_gather(ln1_bias, "wt", axis=0, tiled=True),
        lax.all_gather(w_qkv, "wt", axis=0, tiled=True),
        lax.all_gather(bias_q, "wt", axis=0, tiled=True),
        lax.all_gather(bias_v, "wt", axis=0, tiled=True),
        lax.all_gather(w_out, "wt", axis=0, tiled=True),
        lax.all_gather(bias_out, "wt", axis=0, tiled=True),
        lax.all_gather(ln2_gain, "wt", axis=0, tiled=True),
        lax.all_gather(ln2_bias, "wt", axis=0, tiled=True),
        lax.all_gather(w_up, "wt", axis=0, tiled=True),
        lax.all_gather(bias_up, "wt", axis=0, tiled=True),
        lax.all_gather(w_down, "wt", axis=0, tiled=True),
        lax.all_gather(bias_down, "wt", axis=0, tiled=True),
    )
    inputs = tokens[0].astype(jnp.float32)
    tok_count = inputs.shape[0]
    half_rows = tok_count // 2
    width = inputs.shape[1]
    device = lax.axis_index("ctx")
    cycle_size = lax.axis_size("ctx")
    own_pos = half_positions(device, cycle_size, half_rows)
    head_scale = HEAD_DIM ** (-0.5)
    gain_one = gain_attn.astype(jnp.float32)
    shift_one = shift_attn.astype(jnp.float32)
    gain_two = gain_ffn.astype(jnp.float32)
    shift_two = shift_ffn.astype(jnp.float32)
    normed_one = norm_rows(inputs, gain_one, shift_one)
    normed_low = normed_one.astype(jnp.bfloat16)
    qkv_bias = jnp.concatenate([query_bias, jnp.zeros_like(query_bias), value_bias]).astype(
        jnp.float32
    )
    qkv_rows = (product(normed_low, whole_qkv) + qkv_bias).astype(jnp.bfloat16)
    queries = qkv_rows[:, :width].reshape(2, half_rows, width)
    keys_own = qkv_rows[:, width : 2 * width].reshape(2, half_rows, width)
    values_own = qkv_rows[:, 2 * width :].reshape(2, half_rows, width)
    state = (
        jnp.full((2, HEADS, half_rows), MASKED_SCORE, jnp.float32),
        jnp.zeros((2, HEADS, half_rows), jnp.float32),
        jnp.zeros((2, HEADS, half_rows, HEAD_DIM), jnp.float32),
    )
    state = absorb(state, 0, queries, own_pos, keys_own[0], values_own[0], own_pos[0])
    state = absorb(state, 1, queries, own_pos, keys_own[1], values_own[1], own_pos[1])
    state = absorb(state, 1, queries, own_pos, keys_own[0], values_own[0], own_pos[0])

    def absorb_turn(cycle_turn, keys_now, values_now, state_now):
        source = (device - cycle_turn) % cycle_size
        key_pos = half_positions(source, cycle_size, half_rows)
        state_now = absorb(state_now, 1, queries, own_pos, keys_now[0], values_now[0], key_pos[0])
        same_half = jnp.where(source < device, 0, 1).astype(jnp.int32)
        return absorb(
            state_now,
            same_half,
            queries,
            own_pos,
            pick(keys_now, same_half),
            pick(values_now, same_half),
            pick(key_pos, same_half),
        )

    def forward_turn(cycle_turn, carried):
        keys_now, values_now, state_now, keys_store, values_store = carried
        keys_now, values_now = from_behind((keys_now, values_now), "ctx", 1)
        state_now = absorb_turn(cycle_turn, keys_now, values_now, state_now)
        return (keys_now, values_now, state_now, keys_store, values_store)

    store_empty = jnp.zeros((1, 1), jnp.bfloat16)
    keys_end, values_end, state, keys_store, values_store = lax.fori_loop(
        1, cycle_size, forward_turn, (keys_own, values_own, state, store_empty, store_empty)
    )
    peaks, totals, sums = state
    attended = sums / totals[..., None]
    log_norm = peaks + jnp.log(totals)
    att_low = jnp.transpose(attended, (0, 2, 1, 3)).reshape(tok_count, width).astype(jnp.bfloat16)
    resid_mid = inputs + product(att_low, whole_out) + out_bias.astype(jnp.float32)
    normed_two = norm_rows(resid_mid, gain_two, shift_two)
    normed_two_low = normed_two.astype(jnp.bfloat16)
    hidden_pre = product(normed_two_low, whole_up) + up_bias.astype(jnp.float32)
    hidden_act, gelu_back = jax.vjp(gelu_tanh, hidden_pre)
    hidden_low = hidden_act.astype(jnp.bfloat16)
    result_rows = resid_mid + product(hidden_low, whole_down) + down_bias.astype(jnp.float32)
    out = result_rows.astype(jnp.bfloat16)[None]
    grad_rows = cotangent[0]
    grad_float = grad_rows.astype(jnp.float32)
    grad_down = product_left(hidden_low, grad_rows)
    grad_down_bias = jnp.sum(grad_float, axis=0)
    grad_hidden = product_right(grad_rows, whole_down)
    grad_pre = gelu_back(grad_hidden)[0].astype(jnp.bfloat16)
    grad_up = product_left(normed_two_low, grad_pre)
    grad_up_bias = jnp.sum(grad_pre.astype(jnp.float32), axis=0)
    grad_normed_two = product_right(grad_pre, whole_up)
    norm_two_out, norm_two_back = jax.vjp(norm_rows, resid_mid, gain_two, shift_two)
    grad_mid_norm, grad_gain_two, grad_shift_two = norm_two_back(grad_normed_two)
    grad_mid = grad_float + grad_mid_norm
    grad_mix_low = grad_mid.astype(jnp.bfloat16)
    grad_out = product_left(att_low, grad_mix_low)
    grad_out_bias = jnp.sum(grad_mix_low.astype(jnp.float32), axis=0)
    grad_att_low = product_right(grad_mix_low, whole_out).astype(jnp.bfloat16)
    grad_att_halves = grad_att_low.reshape(2, half_rows, width)
    grad_att_heads = jnp.transpose(
        grad_att_low.astype(jnp.float32).reshape(2, half_rows, HEADS, HEAD_DIM), (0, 2, 1, 3)
    )
    correction = jnp.sum(grad_att_heads * attended, axis=-1)

    def pair_back(grads_in, query_half, key_half, keys_now, values_now, key_pos):
        grad_q, grad_k, grad_v = grads_in
        query_piece = pick(queries, query_half)
        key_piece = pick(keys_now, key_half)
        value_piece = pick(values_now, key_half)
        grad_piece = pick(grad_att_halves, query_half)
        scores = pair_scores(
            query_piece, key_piece, pick(own_pos, query_half), pick(key_pos, key_half)
        )
        prob_full = jnp.exp(scores - pick(log_norm, query_half)[..., None])
        grad_prob = jnp.einsum(
            "qhd,khd->hqk",
            head_split(grad_piece),
            head_split(value_piece),
            preferred_element_type=jnp.float32,
        )
        grad_score = (prob_full * (grad_prob - pick(correction, query_half)[..., None])).astype(
            jnp.bfloat16
        )
        prob_low = prob_full.astype(jnp.bfloat16)
        part_v = jnp.einsum(
            "hqk,qhd->khd", prob_low, head_split(grad_piece), preferred_element_type=jnp.float32
        )
        part_q = (
            jnp.einsum(
                "hqk,khd->qhd",
                grad_score,
                head_split(key_piece),
                preferred_element_type=jnp.float32,
            )
            * head_scale
        )
        part_k = (
            jnp.einsum(
                "hqk,qhd->khd",
                grad_score,
                head_split(query_piece),
                preferred_element_type=jnp.float32,
            )
            * head_scale
        )
        return (
            put_add(grad_q, query_half, part_q.reshape(half_rows, width)),
            put_add(grad_k, key_half, part_k.reshape(half_rows, width)),
            put_add(grad_v, key_half, part_v.reshape(half_rows, width)),
        )

    zero_half = jnp.zeros((2, half_rows, width), jnp.float32)
    grads_now = (zero_half, zero_half, zero_half)
    grads_now = pair_back(grads_now, 0, 0, keys_own, values_own, own_pos)
    grads_now = pair_back(grads_now, 1, 1, keys_own, values_own, own_pos)
    grads_now = pair_back(grads_now, 1, 0, keys_own, values_own, own_pos)

    def back_pairs(cycle_turn, grads_in, keys_now, values_now):
        source = (device - cycle_turn) % cycle_size
        key_pos = half_positions(source, cycle_size, half_rows)
        grads_in = pair_back(grads_in, 1, 0, keys_now, values_now, key_pos)
        same_half = jnp.where(source < device, 0, 1).astype(jnp.int32)
        return pair_back(grads_in, same_half, same_half, keys_now, values_now, key_pos)

    def backward_turn(cycle_turn, carried):
        keys_now, values_now, grad_q, grad_k, grad_v = carried
        keys_now, values_now = from_behind((keys_now, values_now), "ctx", 1)
        grad_k, grad_v = pass_grads(grad_k, grad_v)
        grad_q, grad_k, grad_v = back_pairs(
            cycle_turn, (grad_q, grad_k, grad_v), keys_now, values_now
        )
        return (keys_now, values_now, grad_q, grad_k, grad_v)

    keys_back, values_back, grad_q, grad_k, grad_v = lax.fori_loop(
        1, cycle_size, backward_turn, (keys_own, values_own) + grads_now
    )
    grad_k, grad_v = pass_grads(grad_k, grad_v)
    grad_qkv = jnp.concatenate(
        [
            grad_q.reshape(tok_count, width),
            grad_k.reshape(tok_count, width),
            grad_v.reshape(tok_count, width),
        ],
        axis=1,
    ).astype(jnp.bfloat16)
    grad_qkv_weight = product_left(normed_low, grad_qkv)
    grad_qkv_float = grad_qkv.astype(jnp.float32)
    grad_query_bias = jnp.sum(grad_qkv_float[:, :width], axis=0)
    grad_value_bias = jnp.sum(grad_qkv_float[:, 2 * width :], axis=0)
    grad_normed_one = product_right(grad_qkv, whole_qkv)
    norm_one_out, norm_one_back = jax.vjp(norm_rows, inputs, gain_one, shift_one)
    grad_in_norm, grad_gain_one, grad_shift_one = norm_one_back(grad_normed_one)
    grad_inputs = (grad_mid + grad_in_norm)[None]
    local_grads = [
        grad_gain_one,
        grad_shift_one,
        grad_qkv_weight,
        grad_query_bias,
        grad_value_bias,
        grad_out,
        grad_out_bias,
        grad_gain_two,
        grad_shift_two,
        grad_up,
        grad_up_bias,
        grad_down,
        grad_down_bias,
    ]
    pieces = (
        lax.psum_scatter(
            local_grads[0].astype(jnp.bfloat16), "wt", scatter_dimension=0, tiled=True
        ).astype(jnp.float32),
        lax.psum_scatter(
            local_grads[1].astype(jnp.bfloat16), "wt", scatter_dimension=0, tiled=True
        ).astype(jnp.float32),
        lax.psum_scatter(
            local_grads[2].astype(jnp.bfloat16), "wt", scatter_dimension=0, tiled=True
        ).astype(jnp.float32),
        lax.psum_scatter(
            local_grads[3].astype(jnp.bfloat16), "wt", scatter_dimension=0, tiled=True
        ).astype(jnp.float32),
        lax.psum_scatter(
            local_grads[4].astype(jnp.bfloat16), "wt", scatter_dimension=0, tiled=True
        ).astype(jnp.float32),
        lax.psum_scatter(
            local_grads[5].astype(jnp.bfloat16), "wt", scatter_dimension=0, tiled=True
        ).astype(jnp.float32),
        lax.psum_scatter(
            local_grads[6].astype(jnp.bfloat16), "wt", scatter_dimension=0, tiled=True
        ).astype(jnp.float32),
        lax.psum_scatter(
            local_grads[7].astype(jnp.bfloat16), "wt", scatter_dimension=0, tiled=True
        ).astype(jnp.float32),
        lax.psum_scatter(
            local_grads[8].astype(jnp.bfloat16), "wt", scatter_dimension=0, tiled=True
        ).astype(jnp.float32),
        lax.psum_scatter(
            local_grads[9].astype(jnp.bfloat16), "wt", scatter_dimension=0, tiled=True
        ).astype(jnp.float32),
        lax.psum_scatter(
            local_grads[10].astype(jnp.bfloat16), "wt", scatter_dimension=0, tiled=True
        ).astype(jnp.float32),
        lax.psum_scatter(
            local_grads[11].astype(jnp.bfloat16), "wt", scatter_dimension=0, tiled=True
        ).astype(jnp.float32),
        lax.psum_scatter(
            local_grads[12].astype(jnp.bfloat16), "wt", scatter_dimension=0, tiled=True
        ).astype(jnp.float32),
    )
    owned = (
        lax.psum(pieces[0].astype(jnp.bfloat16), "ctx").astype(jnp.float32),
        lax.psum(pieces[1].astype(jnp.bfloat16), "ctx").astype(jnp.float32),
        lax.psum(pieces[2].astype(jnp.bfloat16), "ctx").astype(jnp.float32),
        lax.psum(pieces[3].astype(jnp.bfloat16), "ctx").astype(jnp.float32),
        lax.psum(pieces[4].astype(jnp.bfloat16), "ctx").astype(jnp.float32),
        lax.psum(pieces[5].astype(jnp.bfloat16), "ctx").astype(jnp.float32),
        lax.psum(pieces[6].astype(jnp.bfloat16), "ctx").astype(jnp.float32),
        lax.psum(pieces[7].astype(jnp.bfloat16), "ctx").astype(jnp.float32),
        lax.psum(pieces[8].astype(jnp.bfloat16), "ctx").astype(jnp.float32),
        lax.psum(pieces[9].astype(jnp.bfloat16), "ctx").astype(jnp.float32),
        lax.psum(pieces[10].astype(jnp.bfloat16), "ctx").astype(jnp.float32),
        lax.psum(pieces[11].astype(jnp.bfloat16), "ctx").astype(jnp.float32),
        lax.psum(pieces[12].astype(jnp.bfloat16), "ctx").astype(jnp.float32),
    )
    return (
        out,
        grad_inputs,
        owned[0],
        owned[1],
        owned[2],
        owned[3],
        owned[4],
        owned[5],
        owned[6],
        owned[7],
        owned[8],
        owned[9],
        owned[10],
        owned[11],
        owned[12],
    )


def solution(mesh):
    return jax.shard_map(
        per_device,
        mesh=mesh,
        in_specs=(
            P("wt", "ctx", None),
            P("wt", "ctx", None),
            P("wt"),
            P("wt"),
            P("wt", None),
            P("wt"),
            P("wt"),
            P("wt", None),
            P("wt"),
            P("wt"),
            P("wt"),
            P("wt", None),
            P("wt"),
            P("wt", None),
            P("wt"),
        ),
        out_specs=(
            P("wt", "ctx", None),
            P("wt", "ctx", None),
            P("wt"),
            P("wt"),
            P("wt", None),
            P("wt"),
            P("wt"),
            P("wt", None),
            P("wt"),
            P("wt"),
            P("wt"),
            P("wt", None),
            P("wt"),
            P("wt", None),
            P("wt"),
        ),
        check_vma=False,
    )
```

profile of v0, /device:TPU:0, one launch (start us, length us, event | category | flops | bytes accessed | tf_op | source)
XLA Modules:
  0.0 997.8 jit_solution(10324142150106339520)
XLA Ops:
  10.2 9.6 all-gather.4
  51.5 8.4 all_gather.49
  68.0 8.4 all-gather.5
  108.3 138.3 %while.46 = (s32[]{:T(128)}, bf16[2,128,1024]{1,2,0:T(8,128)(2,1)}, bf16[2,128,1024]{1,2,0:T(8,128)(2,1)}, f32[2,16,128]{2,1,0:T(8,128)S(1)}, f32[2,16,128]{2,1,...) while((s32[]{:T(128)}, bf16[2,128,1024]{1,2,0:T(8,128)(2,1)}, ...), condition=%wide.region_13.14_spmd, body=%wide.region_8.13_spmd.sunk | while | flops 138461840 | bytes 21816252 | solution.py:206
  110.8 8.6 collective-permute-done
  128.8 10.3 %collective-permute-done = bf16[2,128,1024]{1,2,0:T(8,128)(2,1)S(1)} collective-permute-done((bf16[2,128,1024]{1,2,0:T(8,128)(2,1)}, bf16[2,128,1024]{1,2,0:T(8,128)(2,1)S(1)}, u32[]{:S(2)}, u32[]{:S(2)}) %collective-permute-start) | collective-permute-done | bytes 524320 | tf_op jit(solution)/shard_map/while/body/eval_jaxpr/ppermute | solution.py:17
  148.5 10.3 %collective-permute-done = bf16[2,128,1024]{1,2,0:T(8,128)(2,1)S(1)} collective-permute-done((bf16[2,128,1024]{1,2,0:T(8,128)(2,1)}, bf16[2,128,1024]{1,2,0:T(8,128)(2,1)S(1)}, u32[]{:S(2)}, u32[]{:S(2)}) %collective-permute-start) | collective-permute-done | bytes 524320 | tf_op jit(solution)/shard_map/while/body/eval_jaxpr/ppermute | solution.py:17
  168.1 10.3 %collective-permute-done = bf16[2,128,1024]{1,2,0:T(8,128)(2,1)S(1)} collective-permute-done((bf16[2,128,1024]{1,2,0:T(8,128)(2,1)}, bf16[2,128,1024]{1,2,0:T(8,128)(2,1)S(1)}, u32[]{:S(2)}, u32[]{:S(2)}) %collective-permute-start) | collective-permute-done | bytes 524320 | tf_op jit(solution)/shard_map/while/body/eval_jaxpr/ppermute | solution.py:17
  187.8 10.3 %collective-permute-done = bf16[2,128,1024]{1,2,0:T(8,128)(2,1)S(1)} collective-permute-done((bf16[2,128,1024]{1,2,0:T(8,128)(2,1)}, bf16[2,128,1024]{1,2,0:T(8,128)(2,1)S(1)}, u32[]{:S(2)}, u32[]{:S(2)}) %collective-permute-start) | collective-permute-done | bytes 524320 | tf_op jit(solution)/shard_map/while/body/eval_jaxpr/ppermute | solution.py:17
  207.5 10.3 %collective-permute-done = bf16[2,128,1024]{1,2,0:T(8,128)(2,1)S(1)} collective-permute-done((bf16[2,128,1024]{1,2,0:T(8,128)(2,1)}, bf16[2,128,1024]{1,2,0:T(8,128)(2,1)S(1)}, u32[]{:S(2)}, u32[]{:S(2)}) %collective-permute-start) | collective-permute-done | bytes 524320 | tf_op jit(solution)/shard_map/while/body/eval_jaxpr/ppermute | solution.py:17
  227.2 10.3 %collective-permute-done = bf16[2,128,1024]{1,2,0:T(8,128)(2,1)S(1)} collective-permute-done((bf16[2,128,1024]{1,2,0:T(8,128)(2,1)}, bf16[2,128,1024]{1,2,0:T(8,128)(2,1)S(1)}, u32[]{:S(2)}, u32[]{:S(2)}) %collective-permute-start) | collective-permute-done | bytes 524320 | tf_op jit(solution)/shard_map/while/body/eval_jaxpr/ppermute | solution.py:17
  251.6 8.8 convolution_add_fusion.2
  260.4 38.1 %all-gather.19.cloned.1.call-done = bf16[4096,1024]{1,0:T(8,128)(2,1)} async-done(((bf16[1024,1024]{1,0:T(8,128)(2,1)}), bf16[4096,1024]{1,0:T(8,128)(2,1)}) %all-gather.19.cloned.1.call-update) | async-done | bytes 8388624 | tf_op jit(solution)/shard_map/all_gather | solution.py:151
  298.6 11.7 %fusion.139 = (bf16[4096]{0:T(1024)(128)(2,1)S(1)}, bf16[256,4096]{1,0:T(8,128)(2,1)S(1)}) fusion(f32[256,4096]{1,0:T(8,128)} %convolution_add_fusion.2, bf16[4096,1024]{1,0:T(8,128)(2,1)} %all-gather.19.cloned.1.call-done, bf16[1,256,1024]{2,1,0:T(8,128)(2,1)S(1)} %copy-done.21), kind=kOutput, calls=%fused_computation.278 | convolution fusion | flops 2169499648 | bytes 15212544 | tf_op jit(solution)/shard_map/dot_general | solution.py:42
  351.5 221.3 %while.47 = (s32[]{:T(128)}, bf16[2,128,1024]{1,2,0:T(8,128)(2,1)}, bf16[2,128,1024]{1,2,0:T(8,128)(2,1)}, f32[2,128,1024]{1,2,0:T(8,128)}, f32[2,128,1024]{1,2,...) while((s32[]{:T(128)}, bf16[2,128,1024]{1,2,0:T(8,128)(2,1)}, ...), condition=%wide.region_20.21_spmd, body=%wide.region_19.20_spmd.sunk | while | flops 341607040 | bytes 55223388 | solution.py:312
  575.5 8.9 collective-permute-done.7
  605.1 8.5 convolution_convert_fusion
  614.2 8.3 all-gather.7
  624.5 38.5 %reduce-scatter.5.cloned.1.call-done = bf16[256,3072]{1,0:T(8,128)(2,1)} async-done(((bf16[1024,3072]{1,0:T(8,128)(2,1)}), bf16[256,3072]{1,0:T(8,128)(2,1)}) %reduce-scatter.5.cloned.1.call-update) | async-done | bytes 1572880 | tf_op jit(solution)/shard_map/reduce_scatter | solution.py:354
  663.0 89.4 %reduce-scatter.9.cloned.1.call-done = bf16[256,4096]{1,0:T(8,128)(2,1)} async-done(((bf16[1024,4096]{1,0:T(8,128)(2,1)}), bf16[256,4096]{1,0:T(8,128)(2,1)}) %reduce-scatter.9.cloned.1.call-update) | async-done | bytes 2097168 | tf_op jit(solution)/shard_map/reduce_scatter | solution.py:375
  752.4 89.4 %reduce-scatter.11.cloned.1.call-done = bf16[1024,1024]{1,0:T(8,128)(2,1)} async-done(((bf16[4096,1024]{1,0:T(8,128)(2,1)}), bf16[1024,1024]{1,0:T(8,128)(2,1)}) %reduce-scatter.11.cloned.1.call-update) | async-done | bytes 2097168 | tf_op jit(solution)/shard_map/reduce_scatter | solution.py:381
  856.3 15.6 %all-reduce.11 = (bf16[1024]{0:T(1024)(128)(2,1)S(1)}, bf16[1024]{0:T(1024)(128)(2,1)S(1)}, bf16[1024]{0:T(1024)(128)(2,1)S(1)}, bf16[1024]{0:T(1024)(128)(2,1)S...) all-reduce(bf16[1024]{0:T(1024)(128)(2,1)S(1)} %get-tuple-element.6, ...), channel_id=2, replica_groups=mesh['ctx'=8,'wt'=4] {'wt'}, use_global_device_ids=true, to_apply=%region_24.25.clone | all-reduce | flops 12288 | bytes 49152
  872.5 14.9 %all-reduce.9 = (bf16[256]{0:T(256)(128)(2,1)S(1)}, bf16[256]{0:T(256)(128)(2,1)S(1)}, bf16[256]{0:T(256)(128)(2,1)S(1)}, bf16[256]{0:T(256)(128)(2,1)S(1)}, bf1...) all-reduce(bf16[256]{0:T(256)(128)(2,1)S(1)} %dynamic-slice.1, ...), channel_id=1, replica_groups=mesh['ctx'=8,'wt'=4] {'ctx'}, use_global_device_ids=true, to_apply=%region_25.26 | all-reduce | flops 3072 | bytes 12288 | tf_op jit(solution)/shard_map/psum | solution.py:389
  894.0 87.1 %all-reduce.14.cloned.1.call-done = (bf16[256,3072]{1,0:T(8,128)(2,1)}, bf16[256,1024]{1,0:T(8,128)(2,1)}, bf16[256,4096]{1,0:T(8,128)(2,1)}, bf16[1024,1024]{1,0:T(8,128)(2,1)}) async-done(((bf16[256,3072]{1,0:T(8,128)(2,1)}, bf16[256,1024]{1,0:T(8,128)(2,1)}, bf16[256,4096]{1,0:T(8,128)(2,1)}, bf16[1024,1024]{1,0:T(8,128)(2,1)}), (bf16[256,3072]{1,0:T(8,128)(2,1)}, bf16[256,1024]{1,0:T(8,128)(2,1)}, ...) | async-done | bytes 6291472 | tf_op jit(solution)/shard_map/psum | solution.py:391
  (789 shorter events, 462.3 us)
Async XLA Ops:
  7.3 75.7 %all-gather.13.cloned.1.call-start = ((), (), s32[]{:S(2)}) async-start(), calls=%async_computation.4 | async-start | bytes 7864320 | tf_op jit(solution)/shard_map/all_gather | solution.py:142
  8.0 240.7 %all-gather.15.cloned.1.call-start = ((), (), s32[]{:S(2)}) async-start(), calls=%async_computation.5 | async-start | bytes 2621440 | tf_op jit(solution)/shard_map/all_gather | solution.py:145
  8.8 242.8 %all-gather.17.cloned.1.call-start = ((), (), s32[]{:S(2)}) async-start(), calls=%async_computation.6 | async-start | bytes 10485760 | tf_op jit(solution)/shard_map/all_gather | solution.py:149
  9.5 289.1 %all-gather.19.cloned.1.call-start = ((), (), s32[]{:S(2)}) async-start(), calls=%async_computation.7 | async-start | bytes 10485760 | tf_op jit(solution)/shard_map/all_gather | solution.py:151
  10.1 614.4 %reduce-scatter.7.cloned.1.call-start = ((), (), s32[]{:S(2)}) async-start(), calls=%async_computation.9 | async-start | bytes 2621440 | tf_op jit(solution)/shard_map/reduce_scatter | solution.py:363
  347.3 315.6 %reduce-scatter.5.cloned.1.call-start = ((), (), s32[]{:S(2)}) async-start(), calls=%async_computation.8 | async-start | bytes 7864320 | tf_op jit(solution)/shard_map/reduce_scatter | solution.py:354
  354.2 19.5 %collective-permute-start.4 = (bf16[2,128,1024]{1,2,0:T(8,128)(2,1)}, bf16[2,128,1024]{1,2,0:T(8,128)(2,1)}, u32[]{:S(2)}, u32[]{:S(2)}) collective-permute-start(bf16[2,128,1024]{1,2,0:T(8,128)(2,1)} %convert_element_type.480), channel_id=1, source_target_pairs={{0,4},{4,8},{8,12},{12,16},{16,20},{20,24},{24,28},{28,0},{1,5},{5... | collective-permute-start | bytes 1572872 | tf_op jit(solution)/shard_map/while/body/eval_jaxpr/ppermute | solution.py:17
  355.2 24.1 %collective-permute-start.5 = (bf16[2,128,1024]{1,2,0:T(8,128)(2,1)}, bf16[2,128,1024]{1,2,0:T(8,128)(2,1)}, u32[]{:S(2)}, u32[]{:S(2)}) collective-permute-start(bf16[2,128,1024]{1,2,0:T(8,128)(2,1)} %convert_element_type.482), channel_id=1, source_target_pairs={{0,4},{4,8},{8,12},{12,16},{16,20},{20,24},{24,28},{28,0},{1,5},{5... | collective-permute-start | bytes 1572872 | tf_op jit(solution)/shard_map/while/body/eval_jaxpr/ppermute | solution.py:17
  384.2 21.1 %collective-permute-start.4 = (bf16[2,128,1024]{1,2,0:T(8,128)(2,1)}, bf16[2,128,1024]{1,2,0:T(8,128)(2,1)}, u32[]{:S(2)}, u32[]{:S(2)}) collective-permute-start(bf16[2,128,1024]{1,2,0:T(8,128)(2,1)} %convert_element_type.480), channel_id=1, source_target_pairs={{0,4},{4,8},{8,12},{12,16},{16,20},{20,24},{24,28},{28,0},{1,5},{5... | collective-permute-start | bytes 1572872 | tf_op jit(solution)/shard_map/while/body/eval_jaxpr/ppermute | solution.py:17
  385.1 25.8 %collective-permute-start.5 = (bf16[2,128,1024]{1,2,0:T(8,128)(2,1)}, bf16[2,128,1024]{1,2,0:T(8,128)(2,1)}, u32[]{:S(2)}, u32[]{:S(2)}) collective-permute-start(bf16[2,128,1024]{1,2,0:T(8,128)(2,1)} %convert_element_type.482), channel_id=1, source_target_pairs={{0,4},{4,8},{8,12},{12,16},{16,20},{20,24},{24,28},{28,0},{1,5},{5... | collective-permute-start | bytes 1572872 | tf_op jit(solution)/shard_map/while/body/eval_jaxpr/ppermute | solution.py:17
  414.9 16.3 %collective-permute-start.3 = (bf16[2,128,1024]{1,2,0:T(8,128)(2,1)}, bf16[2,128,1024]{1,2,0:T(8,128)(2,1)}, u32[]{:S(2)}, u32[]{:S(2)}) collective-permute-start(bf16[2,128,1024]{1,2,0:T(8,128)(2,1)} %get-tuple-element.1034), channel_id=1, source_target_pairs={{0,4},{4,8},{8,12},{12,16},{16,20},{20,24},{24,28},{28,0},{1,5},{5... | collective-permute-start | bytes 1572872 | tf_op jit(solution)/shard_map/while/body/eval_jaxpr/ppermute | solution.py:17
  415.8 21.1 %collective-permute-start.4 = (bf16[2,128,1024]{1,2,0:T(8,128)(2,1)}, bf16[2,128,1024]{1,2,0:T(8,128)(2,1)}, u32[]{:S(2)}, u32[]{:S(2)}) collective-permute-start(bf16[2,128,1024]{1,2,0:T(8,128)(2,1)} %convert_element_type.480), channel_id=1, source_target_pairs={{0,4},{4,8},{8,12},{12,16},{16,20},{20,24},{24,28},{28,0},{1,5},{5... | collective-permute-start | bytes 1572872 | tf_op jit(solution)/shard_map/while/body/eval_jaxpr/ppermute | solution.py:17
  416.7 25.8 %collective-permute-start.5 = (bf16[2,128,1024]{1,2,0:T(8,128)(2,1)}, bf16[2,128,1024]{1,2,0:T(8,128)(2,1)}, u32[]{:S(2)}, u32[]{:S(2)}) collective-permute-start(bf16[2,128,1024]{1,2,0:T(8,128)(2,1)} %convert_element_type.482), channel_id=1, source_target_pairs={{0,4},{4,8},{8,12},{12,16},{16,20},{20,24},{24,28},{28,0},{1,5},{5... | collective-permute-start | bytes 1572872 | tf_op jit(solution)/shard_map/while/body/eval_jaxpr/ppermute | solution.py:17
  447.3 21.1 %collective-permute-start.4 = (bf16[2,128,1024]{1,2,0:T(8,128)(2,1)}, bf16[2,128,1024]{1,2,0:T(8,128)(2,1)}, u32[]{:S(2)}, u32[]{:S(2)}) collective-permute-start(bf16[2,128,1024]{1,2,0:T(8,128)(2,1)} %convert_element_type.480), channel_id=1, source_target_pairs={{0,4},{4,8},{8,12},{12,16},{16,20},{20,24},{24,28},{28,0},{1,5},{5... | collective-permute-start | bytes 1572872 | tf_op jit(solution)/shard_map/while/body/eval_jaxpr/ppermute | solution.py:17
  448.2 25.8 %collective-permute-start.5 = (bf16[2,128,1024]{1,2,0:T(8,128)(2,1)}, bf16[2,128,1024]{1,2,0:T(8,128)(2,1)}, u32[]{:S(2)}, u32[]{:S(2)}) collective-permute-start(bf16[2,128,1024]{1,2,0:T(8,128)(2,1)} %convert_element_type.482), channel_id=1, source_target_pairs={{0,4},{4,8},{8,12},{12,16},{16,20},{20,24},{24,28},{28,0},{1,5},{5... | collective-permute-start | bytes 1572872 | tf_op jit(solution)/shard_map/while/body/eval_jaxpr/ppermute | solution.py:17
  478.9 21.1 %collective-permute-start.4 = (bf16[2,128,1024]{1,2,0:T(8,128)(2,1)}, bf16[2,128,1024]{1,2,0:T(8,128)(2,1)}, u32[]{:S(2)}, u32[]{:S(2)}) collective-permute-start(bf16[2,128,1024]{1,2,0:T(8,128)(2,1)} %convert_element_type.480), channel_id=1, source_target_pairs={{0,4},{4,8},{8,12},{12,16},{16,20},{20,24},{24,28},{28,0},{1,5},{5... | collective-permute-start | bytes 1572872 | tf_op jit(solution)/shard_map/while/body/eval_jaxpr/ppermute | solution.py:17
  479.8 25.8 %collective-permute-start.5 = (bf16[2,128,1024]{1,2,0:T(8,128)(2,1)}, bf16[2,128,1024]{1,2,0:T(8,128)(2,1)}, u32[]{:S(2)}, u32[]{:S(2)}) collective-permute-start(bf16[2,128,1024]{1,2,0:T(8,128)(2,1)} %convert_element_type.482), channel_id=1, source_target_pairs={{0,4},{4,8},{8,12},{12,16},{16,20},{20,24},{24,28},{28,0},{1,5},{5... | collective-permute-start | bytes 1572872 | tf_op jit(solution)/shard_map/while/body/eval_jaxpr/ppermute | solution.py:17
  510.5 21.1 %collective-permute-start.4 = (bf16[2,128,1024]{1,2,0:T(8,128)(2,1)}, bf16[2,128,1024]{1,2,0:T(8,128)(2,1)}, u32[]{:S(2)}, u32[]{:S(2)}) collective-permute-start(bf16[2,128,1024]{1,2,0:T(8,128)(2,1)} %convert_element_type.480), channel_id=1, source_target_pairs={{0,4},{4,8},{8,12},{12,16},{16,20},{20,24},{24,28},{28,0},{1,5},{5... | collective-permute-start | bytes 1572872 | tf_op jit(solution)/shard_map/while/body/eval_jaxpr/ppermute | solution.py:17
  511.4 25.8 %collective-permute-start.5 = (bf16[2,128,1024]{1,2,0:T(8,128)(2,1)}, bf16[2,128,1024]{1,2,0:T(8,128)(2,1)}, u32[]{:S(2)}, u32[]{:S(2)}) collective-permute-start(bf16[2,128,1024]{1,2,0:T(8,128)(2,1)} %convert_element_type.482), channel_id=1, source_target_pairs={{0,4},{4,8},{8,12},{12,16},{16,20},{20,24},{24,28},{28,0},{1,5},{5... | collective-permute-start | bytes 1572872 | tf_op jit(solution)/shard_map/while/body/eval_jaxpr/ppermute | solution.py:17
  542.0 21.1 %collective-permute-start.4 = (bf16[2,128,1024]{1,2,0:T(8,128)(2,1)}, bf16[2,128,1024]{1,2,0:T(8,128)(2,1)}, u32[]{:S(2)}, u32[]{:S(2)}) collective-permute-start(bf16[2,128,1024]{1,2,0:T(8,128)(2,1)} %convert_element_type.480), channel_id=1, source_target_pairs={{0,4},{4,8},{8,12},{12,16},{16,20},{20,24},{24,28},{28,0},{1,5},{5... | collective-permute-start | bytes 1572872 | tf_op jit(solution)/shard_map/while/body/eval_jaxpr/ppermute | solution.py:17
  542.9 25.8 %collective-permute-start.5 = (bf16[2,128,1024]{1,2,0:T(8,128)(2,1)}, bf16[2,128,1024]{1,2,0:T(8,128)(2,1)}, u32[]{:S(2)}, u32[]{:S(2)}) collective-permute-start(bf16[2,128,1024]{1,2,0:T(8,128)(2,1)} %convert_element_type.482), channel_id=1, source_target_pairs={{0,4},{4,8},{8,12},{12,16},{16,20},{20,24},{24,28},{28,0},{1,5},{5... | collective-permute-start | bytes 1572872 | tf_op jit(solution)/shard_map/while/body/eval_jaxpr/ppermute | solution.py:17
  595.5 156.9 %reduce-scatter.9.cloned.1.call-start = ((), (), s32[]{:S(2)}) async-start(), calls=%async_computation.10 | async-start | bytes 10485760 | tf_op jit(solution)/shard_map/reduce_scatter | solution.py:375
  604.1 237.7 %reduce-scatter.11.cloned.1.call-start = ((), (), s32[]{:S(2)}) async-start(), calls=%async_computation.11 | async-start | bytes 10485760 | tf_op jit(solution)/shard_map/reduce_scatter | solution.py:381
  613.6 367.6 %all-reduce.14.cloned.1.call-start = ((), (), s32[]{:S(2)}) async-start(), calls=%async_computation.12 | async-start | bytes 12582912 | tf_op jit(solution)/shard_map/psum | solution.py:391
  (108 other events, 1854.0 us)
Sparse Core Ops, SparseCore 0:
  9.9 72.9 all-gather.12
  84.8 35.1 all-gather.14
  121.8 87.4 all-gather.16
  211.0 87.4 all-gather.18
  347.4 35.1 reduce-scatter.6
  595.6 67.2 reduce-scatter.4
  666.0 86.3 reduce-scatter.8
  755.4 86.3 reduce-scatter.10
  844.4 136.6 all-reduce.13
where the time goes:
time: 1010 us; the launch traced here: 998 us
  waiting for transfers between devices  595 us (59%)
  matrix products  126 us (12%)
  blocking collectives  104 us (10%)
  local copies, waits for them, and re-layouts  78 us (8%)
  other arithmetic  67.9 us (7%)
  between operations  16.6 us (2%)
    ppermute x44, waiting for transfers between devices, from_behind(): return lax.ppermute(value, axis, pairs)  243 us
    reduce_scatter x1, waiting for transfers between devices, per_device(): lax.psum_scatter(local_grads[9].astype(jnp.bfloat16), 'wt', scatter_dimen...  89.4 us
    reduce_scatter x1, waiting for transfers between devices, per_device(): lax.psum_scatter(local_grads[11].astype(jnp.bfloat16), 'wt', scatter_dime...  89.4 us
    psum x1, waiting for transfers between devices, per_device(): lax.psum(pieces[2].astype(jnp.bfloat16), 'ctx').astype(jnp.float32)  87.1 us
    reduce_scatter x1, waiting for transfers between devices, per_device(): lax.psum_scatter(local_grads[2].astype(jnp.bfloat16), 'wt', scatter_dimen...  38.5 us
    all_gather x1, waiting for transfers between devices, per_device(): lax.all_gather(w_down, 'wt', axis=0, tiled=True)  38.1 us
    while x56, local copies, waits for them, and re-layouts  29.9 us
    dot_general x4, matrix products, product(): return jnp.dot(left, right, preferred_element_type=jnp.float32)  24.3 us
  transfers between devices with their start and end apart: 53, of which 50 were waited for; matrix products, arithmetic and copies ran while one was open for 21% of the time, Pallas kernels for 0%

commit v1 on v0

v1 whole, which is shorter than its diff:
```python
import functools

import jax
import jax.numpy as jnp
import numpy as np
from jax import lax
from jax.experimental import pallas as pl
from jax.experimental.pallas import tpu as pltpu
from jax.sharding import Mesh
from jax.sharding import PartitionSpec as P

HEADS = 16
HEAD_DIM = 64


EPSILON = 1e-05
MASKED_SCORE = -1e30
Q_TILE = 256
K_TILE = 512


def norm_rows(values_in, gain, shift):
    mean_val = jnp.mean(values_in, axis=-1, keepdims=True)
    centred = values_in - mean_val
    spread = jnp.mean(centred * centred, axis=-1, keepdims=True)
    return centred * lax.rsqrt(spread + EPSILON) * gain + shift


def gelu_tanh(values_in):
    return jax.nn.gelu(values_in, approximate=True)


def product(left, right):
    return jnp.dot(left, right, preferred_element_type=jnp.float32)


def product_left(left, right):
    return lax.dot_general(
        left, right, (((0,), (0,)), ((), ())), preferred_element_type=jnp.float32
    )


def product_right(left, right):
    return lax.dot_general(
        left, right, (((1,), (1,)), ((), ())), preferred_element_type=jnp.float32
    )


def tile_allowed(q_start, k_start):
    q_pos = q_start + lax.broadcasted_iota(jnp.int32, (Q_TILE, K_TILE), 0)
    k_pos = k_start + lax.broadcasted_iota(jnp.int32, (Q_TILE, K_TILE), 1)
    return k_pos <= q_pos


def attend_kernel(heads, qkv_ref, att_ref, lse_ref):
    width = heads * HEAD_DIM
    q_start = pl.multiple_of(pl.program_id(0) * Q_TILE, Q_TILE)
    q_rows = pl.ds(q_start, Q_TILE)
    scale = HEAD_DIM ** (-0.5)
    queries = [
        qkv_ref[q_rows, h * HEAD_DIM : (h + 1) * HEAD_DIM] * jnp.bfloat16(scale)
        for h in range(heads)
    ]

    def step(j, carried):
        k_start = pl.multiple_of(j * K_TILE, K_TILE)
        k_rows = pl.ds(k_start, K_TILE)
        allowed = tile_allowed(q_start, k_start)
        new = []
        for h in range(heads):
            peak, total, acc = carried[h]
            at = width + h * HEAD_DIM
            keys = qkv_ref[k_rows, at : at + HEAD_DIM]
            values = qkv_ref[k_rows, at + width : at + width + HEAD_DIM]
            scores = jnp.where(allowed, product_right(queries[h], keys), MASKED_SCORE)
            peak_new = jnp.maximum(peak, jnp.max(scores, axis=-1, keepdims=True))
            fade = jnp.exp(peak - peak_new)
            prob = jnp.exp(scores - peak_new)
            total = total * fade + jnp.sum(prob, axis=-1, keepdims=True)
            acc = acc * fade + product(prob.astype(jnp.bfloat16), values)
            new.append((peak_new, total, acc))
        return tuple(new)

    empty = (
        jnp.full((Q_TILE, 1), MASKED_SCORE, jnp.float32),
        jnp.zeros((Q_TILE, 1), jnp.float32),
        jnp.zeros((Q_TILE, HEAD_DIM), jnp.float32),
    )
    steps = (q_start + Q_TILE + K_TILE - 1) // K_TILE
    done = lax.fori_loop(0, steps, step, (empty,) * heads)
    for h in range(heads):
        peak, total, acc = done[h]
        att_ref[:, h * HEAD_DIM : (h + 1) * HEAD_DIM] = acc / total
        lse_ref[:, h : h + 1] = peak + jnp.log(total)


def attend_back_kernel(heads, qkv_ref, grad_ref, att_ref, lse_ref, out_ref, keys_acc, values_acc):
    width = heads * HEAD_DIM
    index = pl.program_id(0)
    q_start = pl.multiple_of(index * Q_TILE, Q_TILE)
    q_rows = pl.ds(q_start, Q_TILE)
    scale = HEAD_DIM ** (-0.5)

    @pl.when(index == 0)
    def _():
        keys_acc[...] = jnp.zeros_like(keys_acc)
        values_acc[...] = jnp.zeros_like(values_acc)

    queries, grads, norms, deltas = [], [], [], []
    for h in range(heads):
        cols = slice(h * HEAD_DIM, (h + 1) * HEAD_DIM)
        queries.append(qkv_ref[q_rows, cols] * jnp.bfloat16(scale))
        grad = grad_ref[:, cols]
        grads.append(grad)
        norms.append(lse_ref[:, h : h + 1])
        deltas.append(
            jnp.sum(grad.astype(jnp.float32) * att_ref[:, cols], axis=-1, keepdims=True)
        )

    def step(j, carried):
        k_start = pl.multiple_of(j * K_TILE, K_TILE)
        k_rows = pl.ds(k_start, K_TILE)
        allowed = tile_allowed(q_start, k_start)
        new = []
        for h in range(heads):
            cols = slice(h * HEAD_DIM, (h + 1) * HEAD_DIM)
            at = width + h * HEAD_DIM
            keys = qkv_ref[k_rows, at : at + HEAD_DIM]
            values = qkv_ref[k_rows, at + width : at + width + HEAD_DIM]
            scores = jnp.where(allowed, product_right(queries[h], keys), MASKED_SCORE)
            prob = jnp.exp(scores - norms[h])
            grad_prob = product_right(grads[h], values)
            grad_score = (prob * (grad_prob - deltas[h])).astype(jnp.bfloat16)
            values_acc[k_rows, cols] += product_left(prob.astype(jnp.bfloat16), grads[h])
            keys_acc[k_rows, cols] += product_left(grad_score, queries[h])
            new.append(carried[h] + product(grad_score, keys))
        return tuple(new)

    steps = (q_start + Q_TILE + K_TILE - 1) // K_TILE
    zero = jnp.zeros((Q_TILE, HEAD_DIM), jnp.float32)
    done = lax.fori_loop(0, steps, step, (zero,) * heads)
    for h in range(heads):
        out_ref[q_rows, h * HEAD_DIM : (h + 1) * HEAD_DIM] = (done[h] * scale).astype(
            jnp.bfloat16
        )

    @pl.when(index == pl.num_programs(0) - 1)
    def _():
        out_ref[:, width : 2 * width] = keys_acc[...].astype(jnp.bfloat16)
        out_ref[:, 2 * width :] = values_acc[...].astype(jnp.bfloat16)


def attend(qkv, heads):
    rows, width = qkv.shape[0], heads * HEAD_DIM
    work = rows * rows // 2 * heads
    return pl.pallas_call(
        functools.partial(attend_kernel, heads),
        grid=(rows // Q_TILE,),
        in_specs=[pl.BlockSpec((rows, 3 * width), lambda i: (0, 0))],
        out_specs=[
            pl.BlockSpec((Q_TILE, width), lambda i: (i, 0)),
            pl.BlockSpec((Q_TILE, heads), lambda i: (i, 0)),
        ],
        out_shape=[
            jax.ShapeDtypeStruct((rows, width), jnp.float32),
            jax.ShapeDtypeStruct((rows, heads), jnp.float32),
        ],
        compiler_params=pltpu.CompilerParams(vmem_limit_bytes=40 << 20),
        cost_estimate=pl.CostEstimate(
            flops=work * 1024, bytes_accessed=rows * width * 10, transcendentals=work
        ),
    )(qkv)


def attend_back(qkv, grad, att, lse, heads):
    rows, width = qkv.shape[0], heads * HEAD_DIM
    work = rows * rows // 2 * heads
    return pl.pallas_call(
        functools.partial(attend_back_kernel, heads),
        grid=(rows // Q_TILE,),
        in_specs=[
            pl.BlockSpec((rows, 3 * width), lambda i: (0, 0)),
            pl.BlockSpec((Q_TILE, width), lambda i: (i, 0)),
            pl.BlockSpec((Q_TILE, width), lambda i: (i, 0)),
            pl.BlockSpec((Q_TILE, heads), lambda i: (i, 0)),
        ],
        out_specs=pl.BlockSpec((rows, 3 * width), lambda i: (0, 0)),
        out_shape=jax.ShapeDtypeStruct((rows, 3 * width), jnp.bfloat16),
        scratch_shapes=[
            pltpu.VMEM((rows, width), jnp.float32),
            pltpu.VMEM((rows, width), jnp.float32),
        ],
        compiler_params=pltpu.CompilerParams(vmem_limit_bytes=40 << 20),
        cost_estimate=pl.CostEstimate(
            flops=work * 2560, bytes_accessed=rows * width * 20, transcendentals=work
        ),
    )(qkv, grad, att, lse)


def swap(value):
    return lax.ppermute(value, "core", [(0, 1), (1, 0)])


def pair_stack(own, core):
    other = swap(own)
    first = core == 0
    return jnp.stack([jnp.where(first, own, other), jnp.where(first, other, own)])


def pair_sum(partial, core):
    own = lax.dynamic_index_in_dim(partial, core, 0, keepdims=False)
    other = lax.dynamic_index_in_dim(partial, 1 - core, 0, keepdims=False)
    return own + swap(other.astype(jnp.bfloat16)).astype(jnp.float32)


def to_positions(stored, devices, block):
    parts = stored.reshape(devices, 2, block, -1)
    return jnp.concatenate([parts[:, 0], parts[::-1, 1]]).reshape(stored.shape)


def to_stored(ordered, devices, block):
    parts = ordered.reshape(2, devices, block, -1)
    return jnp.stack([parts[0], parts[1, ::-1]], axis=1).reshape(ordered.shape)


def exchange(value):
    return lax.all_to_all(value, "z", split_axis=0, concat_axis=0, tiled=False)


def per_device(
    tokens,
    cotangent,
    ln1_gain,
    ln1_bias,
    w_qkv,
    bias_q,
    bias_v,
    w_out,
    bias_out,
    ln2_gain,
    ln2_bias,
    w_up,
    bias_up,
    w_down,
    bias_down,
):
    core = lax.axis_index("core")
    shards = lax.axis_size("wt")
    chips = lax.axis_size("z")
    devices = 2 * chips
    inputs = tokens[0].astype(jnp.float32)
    tok_count, width = inputs.shape
    block = tok_count // 2
    half = width // 2
    shard = width // shards
    hidden = w_up.shape[1] // 2
    heads = HEADS // devices
    cols = heads * HEAD_DIM

    def half_of(value, axis):
        return lax.dynamic_index_in_dim(value, core, axis, keepdims=False)

    def gather(value):
        return lax.all_gather(value, "wt", axis=0, tiled=True)

    vectors = [ln1_gain, ln1_bias, bias_q, bias_v, bias_out, ln2_gain, ln2_bias, bias_down, bias_up]
    sizes = [v.shape[0] for v in vectors]
    cuts = [sum(sizes[:i]) for i in range(len(sizes) + 1)]
    packed = lax.all_gather(jnp.concatenate(vectors), "wt", axis=0)
    whole = [
        packed[:, a:b].reshape(-1).astype(jnp.float32) for a, b in zip(cuts[:-1], cuts[1:])
    ]
    gain_one, shift_one, query_bias, value_bias, out_bias = whole[:5]
    gain_two, shift_two, down_bias, up_bias = whole[5:]
    query_bias = half_of(query_bias.reshape(shards, 2, -1), 1).reshape(-1)
    value_bias = half_of(value_bias.reshape(shards, 2, -1), 1).reshape(-1)
    up_bias = half_of(up_bias.reshape(shards, 2, -1), 1).reshape(-1)

    half_qkv = gather(half_of(w_qkv.reshape(shard, 3, shards, 2, shard // 2), 3).reshape(shard, -1))
    half_out = gather(half_of(w_out.reshape(2, shard // 2, width), 0))
    half_up = gather(half_of(w_up.reshape(shard, shards, 2, -1), 2).reshape(shard, -1))
    half_down = gather(half_of(w_down.reshape(2, -1, width), 0))

    normed_low = norm_rows(inputs, gain_one, shift_one).astype(jnp.bfloat16)
    normed_pair = pair_stack(normed_low, core).reshape(2 * tok_count, width)
    grad_rows = cotangent[0]
    grad_float = grad_rows.astype(jnp.float32)
    grad_pair = jnp.concatenate([grad_rows, swap(grad_rows)])
    qkv_bias = jnp.concatenate([query_bias, jnp.zeros_like(query_bias), value_bias])
    qkv_rows = (product(normed_pair, half_qkv) + qkv_bias).astype(jnp.bfloat16)
    qkv_sent = jnp.transpose(
        qkv_rows.reshape(2 * tok_count, 3, chips, cols), (2, 0, 1, 3)
    ).reshape(chips, 2 * tok_count, 3 * cols)
    qkv = to_positions(exchange(qkv_sent).reshape(-1, 3 * cols), devices, block)
    attended, log_norm = attend(qkv, heads)
    att_sent = to_stored(attended.astype(jnp.bfloat16), devices, block)
    att_back = exchange(att_sent.reshape(chips, 2 * tok_count, cols))
    att_low = jnp.transpose(att_back, (1, 0, 2)).reshape(2 * tok_count, half)
    mixed = product(att_low, half_out).reshape(2, tok_count, width)
    resid_mid = inputs + pair_sum(mixed, core) + out_bias
    normed_two_low = norm_rows(resid_mid, gain_two, shift_two).astype(jnp.bfloat16)
    two_pair = jnp.concatenate([normed_two_low, swap(normed_two_low)])
    hidden_pre = product(two_pair, half_up) + up_bias
    hidden_act, gelu_back = jax.vjp(gelu_tanh, hidden_pre)
    hidden_low = hidden_act.astype(jnp.bfloat16)
    grad_down = product_left(hidden_low, grad_pair).astype(jnp.bfloat16)
    grad_down = lax.psum_scatter(grad_down, "wt", scatter_dimension=0, tiled=True)
    grad_pre = gelu_back(product_right(grad_pair, half_down))[0].astype(jnp.bfloat16)
    grad_up = product_left(two_pair, grad_pre).astype(jnp.bfloat16)
    grad_up = lax.psum_scatter(grad_up, "wt", scatter_dimension=0, tiled=True)
    grad_up_bias = jnp.sum(grad_pre.astype(jnp.float32), axis=0)
    down_part = product(hidden_low, half_down)
    result_rows = (
        resid_mid
        + down_part[:tok_count]
        + swap(down_part[tok_count:].astype(jnp.bfloat16)).astype(jnp.float32)
        + down_bias
    )
    out = result_rows.astype(jnp.bfloat16)[None]
    back_part = product_right(grad_pre, half_up)
    grad_normed_two = back_part[:tok_count] + swap(
        back_part[tok_count:].astype(jnp.bfloat16)
    ).astype(jnp.float32)
    norm_two_out, norm_two_back = jax.vjp(norm_rows, resid_mid, gain_two, shift_two)
    grad_mid_norm, grad_gain_two, grad_shift_two = norm_two_back(grad_normed_two)
    grad_mid = grad_float + grad_mid_norm
    grad_mix_low = grad_mid.astype(jnp.bfloat16)
    mix_pair = pair_stack(grad_mix_low, core).reshape(2 * tok_count, width)
    grad_att_low = product_right(mix_pair, half_out).astype(jnp.bfloat16)
    grad_out = product_left(att_low, mix_pair).astype(jnp.bfloat16)
    grad_out = lax.psum_scatter(grad_out, "wt", scatter_dimension=0, tiled=True)
    grad_att_sent = jnp.transpose(grad_att_low.reshape(2 * tok_count, chips, cols), (1, 0, 2))
    grad_att = to_positions(exchange(grad_att_sent).reshape(-1, cols), devices, block)
    grad_heads = attend_back(qkv, grad_att, attended, log_norm, heads)
    grad_sent = to_stored(grad_heads, devices, block)
    grad_back = exchange(grad_sent.reshape(chips, 2 * tok_count, 3 * cols))
    grad_qkv = jnp.transpose(
        grad_back.reshape(chips, 2 * tok_count, 3, cols), (1, 2, 0, 3)
    ).reshape(2 * tok_count, 3 * half)
    grad_normed_one = pair_sum(
        product_right(grad_qkv, half_qkv).reshape(2, tok_count, width), core
    )
    norm_one_out, norm_one_back = jax.vjp(norm_rows, inputs, gain_one, shift_one)
    grad_in_norm, grad_gain_one, grad_shift_one = norm_one_back(grad_normed_one)
    grad_inputs = (grad_mid + grad_in_norm)[None]
    grad_qkv_weight = product_left(normed_pair, grad_qkv).astype(jnp.bfloat16)
    qkv_sums = jnp.sum(grad_qkv.astype(jnp.float32), axis=0)

    def half_in(value):
        value = value.reshape(shards, 1, -1)
        mask = jnp.arange(2).reshape(1, 2, 1) == core
        return jnp.where(mask, value, 0.0)

    vector_grads = [
        grad_gain_one,
        grad_shift_one,
        half_in(qkv_sums[:half]),
        half_in(qkv_sums[2 * half :]),
        jnp.sum(grad_mix_low.astype(jnp.float32), axis=0),
        grad_gain_two,
        grad_shift_two,
        jnp.sum(grad_float, axis=0),
        half_in(grad_up_bias),
    ]
    vector_rows = jnp.concatenate([v.reshape(shards, -1) for v in vector_grads], axis=1)
    pad_rows = 16 * (-(-cuts[-1] // (16 * 3 * half)))
    vector_rows = jnp.pad(vector_rows, ((0, 0), (0, pad_rows * 3 * half - cuts[-1])))
    last = jnp.concatenate(
        [
            grad_qkv_weight.reshape(shards, shard, 3 * half),
            vector_rows.reshape(shards, pad_rows, 3 * half).astype(jnp.bfloat16),
        ],
        axis=1,
    ).reshape(-1, 3 * half)
    last = lax.psum_scatter(last, "wt", scatter_dimension=0, tiled=True)
    grad_down, grad_up, grad_out, last = lax.psum((grad_down, grad_up, grad_out, last), "z")
    own_vector = last[shard:]
    vector = (own_vector.astype(jnp.float32) + swap(own_vector).astype(jnp.float32)).reshape(-1)
    vector_out = [vector[a:b] for a, b in zip(cuts[:-1], cuts[1:])]

    def both(value):
        return pair_stack(value, core).astype(jnp.float32)

    down_out = both(grad_down).reshape(-1, width)
    out_out = both(grad_out).reshape(-1, width)
    up_out = jnp.moveaxis(both(grad_up).reshape(2, shard, shards, -1), 0, 2).reshape(shard, -1)
    qkv_out = jnp.moveaxis(
        both(last[:shard]).reshape(2, shard, 3, shards, shard // 2), 0, 3
    ).reshape(shard, -1)
    return (
        out,
        grad_inputs,
        vector_out[0],
        vector_out[1],
        qkv_out,
        vector_out[2],
        vector_out[3],
        out_out,
        vector_out[4],
        vector_out[5],
        vector_out[6],
        up_out,
        vector_out[8],
        down_out,
        vector_out[7],
    )


def solution(mesh):
    count = mesh.shape["ctx"]
    split = Mesh(
        np.asarray(mesh.devices).reshape(count // 2, 2, mesh.shape["wt"]), ("z", "core", "wt")
    )
    return jax.shard_map(
        per_device,
        mesh=split,
        in_specs=(
            P("wt", ("z", "core"), None),
            P("wt", ("z", "core"), None),
            P("wt"),
            P("wt"),
            P("wt", None),
            P("wt"),
            P("wt"),
            P("wt", None),
            P("wt"),
            P("wt"),
            P("wt"),
            P("wt", None),
            P("wt"),
            P("wt", None),
            P("wt"),
        ),
        out_specs=(
            P("wt", ("z", "core"), None),
            P("wt", ("z", "core"), None),
            P("wt"),
            P("wt"),
            P("wt", None),
            P("wt"),
            P("wt"),
            P("wt", None),
            P("wt"),
            P("wt"),
            P("wt"),
            P("wt", None),
            P("wt"),
            P("wt", None),
            P("wt"),
        ),
        check_vma=False,
    )
```

time: 1010 us -> 607 us (0.60)
  waiting for transfers between devices: 595 us -> 329 us
  blocking collectives: 104 us -> 10.4 us
  matrix products: 126 us -> 63.5 us
  Pallas kernels: 0 us -> 47 us
  other arithmetic: 67.9 us -> 33.7 us
  starting transfers between devices: 7.23 us -> 20.5 us
    ppermute x44 -> x13, waiting for transfers between devices: 243 us -> 7.41 us  [swap(): return lax.ppermute(value, 'core', [(0, 1), (1, 0)])]
    reduce_scatter x4, waiting for transfers between devices: 217 us -> 63.4 us  [the longest x1 49.1 us: per_device(): last = lax.psum_scatter(last, 'wt', scatter_dimension=0, tiled=True)]
    all_to_all x0 -> x4, waiting for transfers between devices: none -> 92 us  [exchange(): return lax.all_to_all(value, 'z', split_axis=0, concat_axis=0, tiled=False)]
    all_gather x9 -> x1, blocking collectives: 73.3 us -> 10.4 us  [per_device(): packed = lax.all_gather(jnp.concatenate(vectors), 'wt', axis=0)]
    dot_general x116 -> x0, matrix products: 59.4 us -> none  [the longest x31 14.6 us: pair_scores(): jnp.einsum('qhd,khd->hqk', head_split(query_half), head_split(key_half),...]
    pallas_call x0 -> x2, Pallas kernels: none -> 47 us  [the longest x1 26.9 us: attend_back(): pl.pallas_call(functools.partial(attend_back_kernel, heads), grid=(rows /...]
    convert_element_type x51 -> x6, other arithmetic: 45.7 us -> 5.14 us  [the longest x2 3.74 us: both(): return pair_stack(value, core).astype(jnp.float32)]
    psum x1, waiting for transfers between devices: 87.1 us -> 124 us  [per_device(): lax.psum((grad_down, grad_up, grad_out, last), 'z')]
  transfers between devices with their start and end apart: 53 -> 26, of which waited for: 50 -> 15; matrix products, arithmetic and copies ran while one was open for 21% -> 22% of each run, Pallas kernels for 0% -> 8%
where the time goes in v1:
time: 607 us; the launch traced here: 598 us
  waiting for transfers between devices  329 us (54%)
  local copies, waits for them, and re-layouts  78.9 us (13%)
  matrix products  63.5 us (10%)
  Pallas kernels  47 us (8%)
  other arithmetic  33.7 us (6%)
  starting transfers between devices  20.5 us (3%)
  between operations  15.1 us (2%)
  blocking collectives  10.4 us (2%)
    psum x1, waiting for transfers between devices, per_device(): lax.psum((grad_down, grad_up, grad_out, last), 'z')  124 us
    all_to_all x4, waiting for transfers between devices, exchange(): return lax.all_to_all(value, 'z', split_axis=0, concat_axis=0, tiled=False)  92 us
    reduce_scatter x1, waiting for transfers between devices, per_device(): last = lax.psum_scatter(last, 'wt', scatter_dimension=0, tiled=True)  49.1 us
    all_gather x4, waiting for transfers between devices, gather(): return lax.all_gather(value, 'wt', axis=0, tiled=True)  42.3 us
    pallas_call x1, Pallas kernels, attend_back(): pl.pallas_call(functools.partial(attend_back_kernel, heads), grid=(rows /...  26.9 us
    dot_general x4, matrix products, product(): return jnp.dot(left, right, preferred_element_type=jnp.float32)  25.5 us
    pallas_call x1, Pallas kernels, attend(): pl.pallas_call(functools.partial(attend_kernel, heads), grid=(rows // Q_T...  20.2 us
    dot_general x4, matrix products, product_left(): lax.dot_general(left, right, (((0,), (0,)), ((), ())), preferred_element_...  19.5 us
  transfers between devices with their start and end apart: 26, of which 15 were waited for; matrix products, arithmetic and copies ran while one was open for 22% of the time, Pallas kernels for 8%

profile of v1, /device:TPU:0, one launch (start us, length us, event | category | flops | bytes accessed | tf_op | source)
XLA Modules:
  0.0 598.2 jit_solution(731204711102432010)
XLA Ops:
  7.2 5.1 reshape.331
  12.4 6.4 %dynamic-slice_reduce_fusion = bf16[256,3,4,128]{3,2,1,0:T(4,128)(2,1)S(1)} fusion(bf16[256,3,4,2,128]{4,3,2,1,0:T(2,128)(2,1)} %reshape.331, s32[]{:T(128)S(6)} %select_n.107), kind=kLoop, calls=%fused_computation.32 | loop fusion | bytes 1572868 | tf_op jit(solution)/shard_map/jit(dynamic_index_in_dim)/dynamic_slice | solution.py:261
  29.3 10.4 %all-gather = bf16[12288]{0:T(1024)(128)(2,1)S(1)} all-gather(bf16[3072]{0:T(1024)(128)(2,1)S(1)} %constant_dynamic-update-slice_fusion.9), channel_id=2, replica_groups=mesh['z'=4,'core'=2,'wt'=4] {'wt'}, dimensions={0}, use_global_device_ids=true | all-gather | bytes 30720 | tf_op jit(solution)/shard_map/all_gather | solution.py:269
  45.1 21.8 %all-gather.8.cloned.1.call-done = bf16[1024,1536]{1,0:T(8,128)(2,1)} async-done(((bf16[256,1536]{1,0:T(8,128)(2,1)}), bf16[1024,1536]{1,0:T(8,128)(2,1)}) %all-gather.8.cloned.1.call-update) | async-done | bytes 3145744 | tf_op jit(solution)/shard_map/all_gather | solution.py:264
  66.9 5.1 fusion.13
  79.8 4.6 all-to-all-start
  85.5 35.9 %all-to-all-done = bf16[4,512,384]{1,2,0:T(8,128)(2,1)} async-done(((bf16[4,512,384]{1,2,0:T(8,128)(2,1)}), bf16[4,512,384]{1,2,0:T(8,128)(2,1)}, u32[]{:S(2)}, u32[]{:S(2)}) %all-to-all-start) | async-done | bytes 1572896 | tf_op jit(solution)/shard_map/all_to_all | solution.py:227
  123.7 20.2 %shard_map.262 = (f32[2048,128]{1,0:T(8,128)S(1)}, f32[2048,2]{1,0:T(8,128)S(1)}) custom-call(bf16[2048,384]{1,0:T(8,128)(2,1)S(1)} %bitcast.222), custom_call_target="tpu_custom_call" | custom-call | flops 4294967296 | bytes 2621440 | tf_op jit(solution)/shard_map/pallas_call | solution.py:156
  150.0 14.1 %all-to-all-done.1 = bf16[4,512,128]{2,1,0:T(8,128)(2,1)} async-done(((bf16[4,512,128]{2,1,0:T(8,128)(2,1)}), bf16[4,512,128]{2,1,0:T(8,128)(2,1)}, u32[]{:S(2)}, u32[]{:S(2)}) %all-to-all-start.1) | async-done | bytes 524320 | tf_op jit(solution)/shard_map/all_to_all | solution.py:227
  177.1 6.9 %fusion.36 = f32[512,2048]{1,0:T(8,128)} fusion(bf16[1024,2048]{0,1:T(8,128)(2,1)} %all-gather.10.cloned.1.call-done, bf16[256,1024]{1,0:T(8,128)(2,1)} %collective-permute-done.2, bf16[256,1024]{1,0:T(8,128)(2,1)} %add_convert_fusion), kind=kOutput, calls=%fused_computation.84 | convolution fusion | flops 2149580800 | bytes 9437184 | tf_op jit(solution)/shard_map/dot_general | solution.py:34
  184.0 20.5 %all-gather.14.cloned.1.call-done = bf16[1,2048,1024]{2,1,0:T(8,128)(2,1)} async-done(((bf16[1,512,1024]{2,1,0:T(8,128)(2,1)}), bf16[1,2048,1024]{2,1,0:T(8,128)(2,1)}) %all-gather.14.cloned.1.call-update) | async-done | bytes 4194320 | tf_op jit(solution)/shard_map/all_gather | solution.py:264
  204.5 8.7 %convert_reduce_fusion = (bf16[2048]{0:T(1024)(128)(2,1)S(1)}, bf16[512,2048]{1,0:T(8,128)(2,1)S(1)}) fusion(f32[512,2048]{1,0:T(8,128)} %fusion.36, f32[2048]{0:T(1024)S(1)} %bitcast.268, bf16[1,2048,1024]{2,1,0:T(8,128)(2,1)} %all-gather.14.cloned.1.call-done, bf16[256,1024]{1,0:T(8,128)(2,1)} %collective-permute-done.4, bf16[256,1024]{1,0:T(8,128)(2,1)} %bitcast.29), kind=kOutput, calls=%fused_computation.14 | convolution fusion | flops 2173696000 | bytes 11546624 | tf_op jit(solution)/shard_map/dot_general | solution.py:44
  217.4 11.4 %fusion.9 = f32[512,1024]{1,0:T(8,128)S(1)} fusion(bf16[1,2048,1024]{2,1,0:T(8,128)(2,1)S(1)} %copy-done.27, f32[512,2048]{1,0:T(8,128)S(1)} %copy-done.28, f32[2048]{0:T(1024)S(1)} %bitcast.269), kind=kOutput, calls=%fused_computation.11 | convolution fusion | flops 2157969408 | bytes 10493952 | tf_op jit(solution)/shard_map/dot_general | solution.py:34
  241.7 6.3 %convolution_convert_fusion.1 = bf16[1024,2048]{1,0:T(8,128)(2,1)} fusion(bf16[512,2048]{1,0:T(8,128)(2,1)} %copy-done.29, bf16[256,1024]{1,0:T(8,128)(2,1)} %collective-permute-done.2, bf16[256,1024]{1,0:T(8,128)(2,1)} %add_convert_fusion), kind=kOutput, calls=%fused_computation.17 | convolution fusion | flops 2151677952 | bytes 7340032 | tf_op jit(solution)/shard_map/dot_general | solution.py:38
  253.2 4.7 all-to-all-start.2
  257.9 7.9 %convolution_convert_fusion = bf16[2048,1024]{1,0:T(8,128)(2,1)} fusion(bf16[256,1024]{1,0:T(8,128)(2,1)} %collective-permute-done.4, bf16[256,1024]{1,0:T(8,128)(2,1)} %bitcast.29, f32[512,2048]{1,0:T(8,128)} %fusion.36, f32[2048]{0:T(1024)S(1)} %bitcast.270), kind=kOutput, calls=%fused_computation.16 | convolution fusion | flops 2162163712 | bytes 9445376 | tf_op jit(solution)/shard_map/dot_general | solution.py:38
  265.8 7.1 %all-to-all-done.2 = bf16[4,512,128]{2,1,0:T(8,128)(2,1)} async-done(((bf16[4,512,128]{2,1,0:T(8,128)(2,1)}), bf16[4,512,128]{2,1,0:T(8,128)(2,1)}, u32[]{:S(2)}, u32[]{:S(2)}) %all-to-all-start.2) | async-done | bytes 524320 | tf_op jit(solution)/shard_map/all_to_all | solution.py:227
  275.3 26.9 %shard_map.263 = bf16[2048,384]{1,0:T(8,128)(2,1)S(1)} custom-call(bf16[2048,384]{1,0:T(8,128)(2,1)S(1)} %bitcast.223, bf16[2048,128]{1,0:T(8,128)(2,1)S(1)} %bitcast.224, f32[2048,128]{1,0:T(8,128)S(1)} %get-tuple-element.17.att_ref, f32[2048,2]{1,0:T(8,128)S(1)} %copy-done.3), custom_call_target="tpu_custom_call" | custom-call | flops 10737418240 | bytes 5242880 | tf_op jit(solution)/shard_map/pallas_call | solution.py:178
  309.8 35.0 %all-to-all-done.3 = bf16[4,512,384]{2,1,0:T(8,128)(2,1)} async-done(((bf16[4,512,384]{2,1,0:T(8,128)(2,1)}), bf16[4,512,384]{2,1,0:T(8,128)(2,1)}, u32[]{:S(2)}, u32[]{:S(2)}) %all-to-all-start.3) | async-done | bytes 1572896 | tf_op jit(solution)/shard_map/all_to_all | solution.py:227
  367.3 14.2 %reduce-scatter.11.cloned.1.call-done = bf16[512,1024]{1,0:T(8,128)(2,1)} async-done(((bf16[2048,1024]{1,0:T(8,128)(2,1)}), bf16[512,1024]{1,0:T(8,128)(2,1)}) %reduce-scatter.11.cloned.1.call-update) | async-done | bytes 1048592 | tf_op jit(solution)/shard_map/reduce_scatter | solution.py:307
  381.4 49.1 %reduce-scatter.5.cloned.1.call-done = bf16[272,1536]{1,0:T(8,128)(2,1)} async-done(((bf16[1088,1536]{1,0:T(8,128)(2,1)}), bf16[272,1536]{1,0:T(8,128)(2,1)}) %reduce-scatter.5.cloned.1.call-update) | async-done | bytes 835600 | tf_op jit(solution)/shard_map/reduce_scatter | solution.py:375
  432.4 123.7 %all-reduce.4.cloned.1.call-done = (bf16[272,1536]{1,0:T(8,128)(2,1)}, bf16[128,1024]{1,0:T(8,128)(2,1)}, bf16[256,2048]{1,0:T(8,128)(2,1)}, bf16[512,1024]{1,0:T(8,128)(2,1)}) async-done(((bf16[272,1536]{1,0:T(8,128)(2,1)}, bf16[128,1024]{1,0:T(8,128)(2,1)}, bf16[256,2048]{1,0:T(8,128)(2,1)}, bf16[512,1024]{1,0:T(8,128)(2,1)}), (bf16[272,1536]{1,0:T(8,128)(2,1)}, bf16[128,1024]{1,0:T(8,128)(2,1)}, ...) | async-done | bytes 3194896 | tf_op jit(solution)/shard_map/psum | solution.py:376
  574.8 5.3 copy.81
  580.1 6.6 %reshape.374 = f32[256,4096]{1,0:T(8,128)} reshape(f32[256,4,2,512]{3,2,1,0:T(2,128)} %copy.81) | data formatting | bytes 8388608 | tf_op jit(solution)/shard_map/reshape | solution.py:386
  (251 shorter events, 125.1 us)
Async XLA Ops:
  7.2 59.7 %all-gather.8.cloned.1.call-start = ((), (), s32[]{:S(2)}) async-start(), calls=%async_computation.8 | async-start | bytes 3932160 | tf_op jit(solution)/shard_map/all_gather | solution.py:264
  20.0 148.3 %all-gather.12.cloned.1.call-start = ((), (), s32[]{:S(2)}) async-start(), calls=%async_computation.14 | async-start | bytes 1310720 | tf_op jit(solution)/shard_map/all_gather | solution.py:264
  21.0 154.5 %all-gather.10.cloned.1.call-start = ((), (), s32[]{:S(2)}) async-start(), calls=%async_computation.9 | async-start | bytes 5242880 | tf_op jit(solution)/shard_map/all_gather | solution.py:264
  40.5 2.1 collective-permute-start
  79.8 41.5 %all-to-all-start = ((bf16[4,512,384]{1,2,0:T(8,128)(2,1)}), bf16[4,512,384]{1,2,0:T(8,128)(2,1)}, u32[]{:S(2)}, u32[]{:S(2)}) async-start(bf16[4,512,384]{1,2,0:T(8,128)(2,1)} %bitcast.230), calls=%async_computation | async-start | bytes 3145728 | tf_op jit(solution)/shard_map/all_to_all | solution.py:227
  84.4 120.1 %all-gather.14.cloned.1.call-start = ((), (), s32[]{:S(2)}) async-start(), calls=%async_computation.15 | async-start | bytes 5242880 | tf_op jit(solution)/shard_map/all_gather | solution.py:264
  145.8 18.3 %all-to-all-start.1 = ((bf16[4,512,128]{2,1,0:T(8,128)(2,1)}), bf16[4,512,128]{2,1,0:T(8,128)(2,1)}, u32[]{:S(2)}, u32[]{:S(2)}) async-start(bf16[4,512,128]{2,1,0:T(8,128)(2,1)} %bitcast.240), calls=%async_computation.1 | async-start | bytes 1048576 | tf_op jit(solution)/shard_map/all_to_all | solution.py:227
  150.0 217.3 %reduce-scatter.7.cloned.1.call-start = ((), (), s32[]{:S(2)}) async-start(), calls=%async_computation.11 | async-start | bytes 1310720 | tf_op jit(solution)/shard_map/reduce_scatter | solution.py:331
  174.8 2.3 collective-permute-start.2
  175.0 9.0 %collective-permute-start.4 = (bf16[256,1024]{1,0:T(8,128)(2,1)}, bf16[256,1024]{1,0:T(8,128)(2,1)}, u32[]{:S(2)}, u32[]{:S(2)}) collective-permute-start(bf16[256,1024]{1,0:T(8,128)(2,1)} %bitcast.29), channel_id=1, source_target_pairs={{0,4},{4,0},{1,5},{5,1},{2,6},{6,2},{3,7},{7,3},{8,12},{12,8},{9,1... | collective-permute-start | bytes 1572872 | tf_op jit(solution)/shard_map/ppermute | solution.py:201
  215.7 13.3 %collective-permute-start.5 = (bf16[256,1024]{1,0:T(8,128)(2,1)S(1)}, bf16[256,1024]{1,0:T(8,128)(2,1)S(1)}, u32[]{:S(2)}, u32[]{:S(2)}) collective-permute-start(bf16[256,1024]{1,0:T(8,128)(2,1)S(1)} %slice.220), channel_id=1, source_target_pairs={{0,4},{4,0},{1,5},{5,1},{2,6},{6,2},{3,7},{7,3},{8,12},{12,8},{9,1... | collective-permute-start | bytes 1572872 | tf_op jit(solution)/shard_map/ppermute | solution.py:201
  235.3 2.3 collective-permute-start.6
  241.7 125.6 %reduce-scatter.9.cloned.1.call-start = ((), (), s32[]{:S(2)}) async-start(), calls=%async_computation.12 | async-start | bytes 5242880 | tf_op jit(solution)/shard_map/reduce_scatter | solution.py:310
  253.2 19.7 %all-to-all-start.2 = ((bf16[4,512,128]{2,1,0:T(8,128)(2,1)}), bf16[4,512,128]{2,1,0:T(8,128)(2,1)}, u32[]{:S(2)}, u32[]{:S(2)}) async-start(bf16[4,512,128]{2,1,0:T(8,128)(2,1)} %bitcast.239), calls=%async_computation.2 | async-start | bytes 1048576 | tf_op jit(solution)/shard_map/all_to_all | solution.py:227
  257.9 123.5 %reduce-scatter.11.cloned.1.call-start = ((), (), s32[]{:S(2)}) async-start(), calls=%async_computation.13 | async-start | bytes 5242880 | tf_op jit(solution)/shard_map/reduce_scatter | solution.py:307
  303.8 41.0 %all-to-all-start.3 = ((bf16[4,512,384]{2,1,0:T(8,128)(2,1)}), bf16[4,512,384]{2,1,0:T(8,128)(2,1)}, u32[]{:S(2)}, u32[]{:S(2)}) async-start(bf16[4,512,384]{2,1,0:T(8,128)(2,1)} %bitcast.43), calls=%async_computation.3 | async-start | bytes 3145728 | tf_op jit(solution)/shard_map/all_to_all | solution.py:227
  308.1 122.4 %reduce-scatter.5.cloned.1.call-start = ((), (), s32[]{:S(2)}) async-start(), calls=%async_computation.10 | async-start | bytes 4177920 | tf_op jit(solution)/shard_map/reduce_scatter | solution.py:375
  358.4 4.0 collective-permute-start.7
  367.2 189.0 %all-reduce.4.cloned.1.call-start = ((), (), s32[]{:S(2)}) async-start(), calls=%async_computation.16 | async-start | bytes 6389760 | tf_op jit(solution)/shard_map/psum | solution.py:376
  557.0 3.5 collective-permute-start.8
  559.4 4.1 collective-permute-start.9
  560.0 2.3 collective-permute-start.10
  560.0 10.1 %collective-permute-start.11 = (bf16[256,2048]{1,0:T(8,128)(2,1)}, bf16[256,2048]{1,0:T(8,128)(2,1)}, u32[]{:S(2)}, u32[]{:S(2)}) collective-permute-start(bf16[256,2048]{1,0:T(8,128)(2,1)} %get-tuple-element.57), channel_id=1, source_target_pairs={{0,4},{4,0},{1,5},{5,1},{2,6},{6,2},{3,7},{7,3},{8,12},{12,8},{9,1... | collective-permute-start | bytes 3145736 | tf_op jit(solution)/shard_map/ppermute | solution.py:201
  560.5 26.3 %collective-permute-start.12 = (bf16[512,1024]{1,0:T(8,128)(2,1)}, bf16[512,1024]{1,0:T(8,128)(2,1)}, u32[]{:S(2)}, u32[]{:S(2)}) collective-permute-start(bf16[512,1024]{1,0:T(8,128)(2,1)} %get-tuple-element.58), channel_id=1, source_target_pairs={{0,4},{4,0},{1,5},{5,1},{2,6},{6,2},{3,7},{7,3},{8,12},{12,8},{9,1... | collective-permute-start | bytes 3145736 | tf_op jit(solution)/shard_map/ppermute | solution.py:201
  (32 other events, 364.3 us)
Sparse Core Ops, SparseCore 0:
  20.1 46.7 all-gather.7
  68.8 26.4 all-gather.11
  97.7 52.4 all-gather.9
  151.9 52.5 all-gather.13
  241.8 27.9 reduce-scatter.6
  273.2 52.5 reduce-scatter.8
  328.8 52.5 reduce-scatter.10
  385.0 45.4 reduce-scatter.4
  433.2 122.8 all-reduce.3
